TPU v7x, 512 devices: a whole 4x8x8 slice. The times are simulated.
512 devices in a mesh: dop: 16 (over z, core), rng: 32 (over x, y).
Axes of the slice: x: 4, y: 8, z: 8, core: 2. Of those that a mesh axis runs over, the one named last changes fastest.
Arguments:
- cube: bfloat16 [2, 64, 128, 16384], P(None, None, 'dop', 'rng'), may hold values from -200 to 200
- train_blocks: int32 [128, 128], P('dop', 'rng'), may hold values 0 or 1
- guard_blocks: int32 [128], P('rng'), may hold values 0 or 1
- prior_factor: float32 [128, 256, 256], P('dop', 'rng'), may hold values from -1638400 to 1638400, as said below
- steering: float32 [128, 256], P('dop'), may hold values from -6 to 6
Outputs:
- filtered: float32 [2, 128, 16384], P(None, 'dop', 'rng')
- factor: float32 [128, 256, 256], P('dop', 'rng')
Inputs may be any that keep to these rules, and one draw needn't show every extreme that they name: `prior_factor`: upper triangular with a positive diagonal.
All inputs are finite; a program needn't handle non-finite values. No bound on the sum of `train_blocks` or of `guard_blocks` on one device may be relied on, other than what follows from the above.
Results may differ from a plain program's by a relative error of at most 0.0041.
Values may be sent and summed in bfloat16 or wider, within the bound.
A program may use at most 64 MiB of HBM per device.

v0:
```python
import math
import jax
import jax.numpy as jnp
from jax import lax
from jax.sharding import PartitionSpec as P

BLOCK = 128
forgetting = 0.98


def from_behind(block, axis, distance):
    devices = range(lax.axis_size(axis))
    route = [((i - distance) % len(devices), i) for i in devices]
    return lax.ppermute(block, axis, route)


def dft_table(pulses):
    index = jnp.arange(pulses, dtype=jnp.int32)
    product = index[:, None] * index[None, :] % pulses
    angle = product.astype(jnp.float32) * (2.0 * math.pi / pulses)
    cosine = jnp.cos(angle)
    sine = jnp.sin(angle)
    top = jnp.stack([cosine, -sine], axis=1)
    bottom = jnp.stack([sine, cosine], axis=1)
    return jnp.stack([top, bottom], axis=0)


def spectra(pulse_block, table):
    out = jnp.einsum(
        "scpg,sptk->tckg", pulse_block.astype(jnp.float32), table, precision=lax.Precision.HIGHEST
    )
    return out.astype(jnp.bfloat16)


def shards(cube, train_blocks, guard_blocks, prior_factor, steering):
    table = dft_table(cube.shape[2] * lax.axis_size("dop"))
    pulse_block = lax.all_to_all(cube, "dop", split_axis=3, concat_axis=2, tiled=True)
    spectrum = lax.all_to_all(
        spectra(pulse_block, table), "dop", split_axis=2, concat_axis=3, tiled=True
    )
    neighbor = from_behind(spectrum[:, :, 0:1, :], "dop", -1)
    following = jnp.concatenate([spectrum[:, :, 1:, :], neighbor], axis=2)
    vectors = jnp.concatenate([spectrum[0], following[0], spectrum[1], following[1]], axis=0)
    usable = train_blocks * guard_blocks[None, :]
    gate_mask = jnp.repeat(usable, BLOCK, axis=1).astype(jnp.bfloat16)
    masked = vectors * gate_mask[None, :, :]
    gram = jnp.einsum("dkg,ekg->kde", masked, masked, preferred_element_type=jnp.float32)
    half = vectors.shape[0] // 2
    real_part = gram[:, :half, :half] + gram[:, half:, half:]
    cross = gram[:, half:, :half] - gram[:, :half, half:]
    prior_gram = forgetting * jnp.einsum(
        "krd,kre->kde", prior_factor, prior_factor, precision=lax.Precision.HIGHEST
    )
    top = jnp.concatenate([real_part, -cross], axis=2)
    bottom = jnp.concatenate([cross, real_part], axis=2)
    local = jnp.concatenate([top, bottom], axis=1) + prior_gram
    covariance = lax.psum(local, "rng")
    lower = jnp.linalg.cholesky(covariance)
    first = lax.linalg.triangular_solve(lower, steering[:, :, None], left_side=True, lower=True)
    second = lax.linalg.triangular_solve(lower, first, left_side=True, lower=True, transpose_a=True)
    weight = second[:, :, 0] / jnp.sum(first[:, :, 0] * first[:, :, 0], axis=1, keepdims=True)
    rotated = jnp.concatenate([-weight[:, half:], weight[:, :half]], axis=1)
    stacked = jnp.stack([weight, rotated]).astype(jnp.bfloat16)
    filtered = jnp.einsum("skd,dkg->skg", stacked, vectors, preferred_element_type=jnp.float32)
    rows = prior_factor.shape[1]
    start = lax.axis_index("rng") * rows
    factor = lax.dynamic_slice_in_dim(jnp.swapaxes(lower, 1, 2), start, rows, axis=1)
    return (filtered, factor)


def solution(mesh):
    return jax.shard_map(
        shards,
        mesh=mesh,
        in_specs=(
            P(None, None, "dop", "rng"),
            P("dop", "rng"),
            P("rng"),
            P("dop", "rng", None),
            P("dop", None),
        ),
        out_specs=(P(None, "dop", "rng"), P("dop", "rng", None)),
        check_vma=False,
    )
```

profile of v0, /device:TPU:64, one launch (start us, length us, event | category | flops | bytes accessed | tf_op | source)
XLA Modules:
  0.0 741.5 jit_solution(6532343640095411719)
XLA Ops:
  7.2 4.0 copy.72
  11.2 2.2 reshape.203
  13.4 10.0 %all-to-all-start = ((bf16[16,2,16384]{2,1,0:T(2,128)(2,1)}), bf16[16,2,16384]{2,1,0:T(2,128)(2,1)S(1)}, u32[]{:S(2)}, u32[]{:S(2)}) async-start(bf16[16,2,16384]{2,1,0:T(2,128)(2,1)} %reshape.203), calls=%async_computation | async-start | bytes 2097152 | tf_op jit(solution)/shard_map/all_to_all | solution.py:37
  24.0 24.0 %all-to-all-done = bf16[16,2,16384]{2,1,0:T(2,128)(2,1)S(1)} async-done(((bf16[16,2,16384]{2,1,0:T(2,128)(2,1)}), bf16[16,2,16384]{2,1,0:T(2,128)(2,1)S(1)}, u32[]{:S(2)}, u32[]{:S(2)}) %all-to-all-start) | async-done | bytes 1048608 | tf_op jit(solution)/shard_map/all_to_all | solution.py:37
  49.4 1.9 copy.74
  51.3 2.9 copy.75
  55.1 3.0 copy.76
  58.2 2.2 reshape.205
  60.4 6.8 all-to-all-start.1
  67.6 24.2 %all-to-all-done.1 = bf16[16,2,16384]{2,1,0:T(2,128)(2,1)S(1)} async-done(((bf16[16,2,16384]{2,1,0:T(2,128)(2,1)}), bf16[16,2,16384]{2,1,0:T(2,128)(2,1)S(1)}, u32[]{:S(2)}, u32[]{:S(2)}) %all-to-all-start.1) | async-done | bytes 1048608 | tf_op jit(solution)/shard_map/all_to_all | solution.py:38
  96.9 3.5 collective-permute-start
  100.4 3.1 fusion.42
  110.5 3.3 maximum_add_fusion
  114.6 164.1 %all-reduce.3.cloned.1.call-done = f32[8,256,256]{1,2,0:T(8,128)} async-done(((f32[8,256,256]{1,2,0:T(8,128)}), f32[8,256,256]{1,2,0:T(8,128)}) %all-reduce.3.cloned.1.call-update) | async-done | bytes 2097168 | tf_op jit(solution)/shard_map/psum | solution.py:57
  278.6 3.1 copy.86
  284.9 93.8 %custom-call.18 = f32[8,128,128]{2,1,0:T(8,128)S(1)} custom-call(f32[8,128,128]{2,1,0:T(8,128)S(1)} %cholesky.122), custom_call_target="Cholesky" | custom-call | tf_op jit(solution)/shard_map/jit(cholesky)/cholesky | solution.py:58
  379.0 79.4 %custom-call.19 = f32[8,1,128,128]{2,3,1,0:T(8,128)} custom-call(f32[8,1,128,128]{3,2,1,0:T(8,128)S(1)} %select_bitcast_fusion), custom_call_target="InvertDiagBlocksLowerTriangular" | custom-call | tf_op jit(solution)/shard_map/jit(cholesky)/cholesky | solution.py:58
  460.2 3.1 convolution_subtract_fusion
  463.3 94.6 %custom-call.20 = f32[8,128,128]{2,1,0:T(8,128)S(1)} custom-call(f32[8,128,128]{2,1,0:T(8,128)} %convolution_subtract_fusion), custom_call_target="Cholesky" | custom-call | tf_op jit(solution)/shard_map/jit(cholesky)/cholesky | solution.py:58
  559.3 3.4 broadcast_select_fusion
  562.8 5.8 while.1
  563.4 2.3 bitcast_dynamic-update-slice_fusion.2
  566.3 2.3 bitcast_dynamic-update-slice_fusion.2
  568.7 158.3 %custom-call.21 = f32[8,2,128,128]{2,3,1,0:T(8,128)S(1)} custom-call(f32[8,2,128,128]{3,2,1,0:T(8,128)} %bitcast.155), custom_call_target="InvertDiagBlocksLowerTriangular" | custom-call | tf_op jit(solution)/shard_map/triangular_solve | solution.py:60
  (99 shorter events, 31.5 us)
Async XLA Ops:
  7.2 103.3 %copy-start = (f32[8,8,256]{2,1,0:T(8,128)S(1)}, f32[8,8,256]{2,1,0:T(8,128)}, u32[]{:S(2)}) copy-start(f32[8,8,256]{2,1,0:T(8,128)} %param.8) | copy-start | bytes 196612
  13.4 34.6 %all-to-all-start = ((bf16[16,2,16384]{2,1,0:T(2,128)(2,1)}), bf16[16,2,16384]{2,1,0:T(2,128)(2,1)S(1)}, u32[]{:S(2)}, u32[]{:S(2)}) async-start(bf16[16,2,16384]{2,1,0:T(2,128)(2,1)} %reshape.203), calls=%async_computation | async-start | bytes 2097152 | tf_op jit(solution)/shard_map/all_to_all | solution.py:37
  58.1 9.3 %copy-start.16 = (s32[8,4]{0,1:T(4,128)S(1)}, s32[8,4]{0,1:T(4,128)}, u32[]{:S(2)}) copy-start(s32[8,4]{0,1:T(4,128)} %param.6) | copy-start | bytes 388
  58.2 9.3 %copy-start.17 = (s32[4]{0:T(128)S(1)}, s32[4]{0:T(128)}, u32[]{:S(2)}) copy-start(s32[4]{0:T(128)} %param.7) | copy-start | bytes 52
  60.4 31.4 %all-to-all-start.1 = ((bf16[16,2,16384]{2,1,0:T(2,128)(2,1)}), bf16[16,2,16384]{2,1,0:T(2,128)(2,1)S(1)}, u32[]{:S(2)}, u32[]{:S(2)}) async-start(bf16[16,2,16384]{2,1,0:T(2,128)(2,1)} %reshape.205), calls=%async_computation.1 | async-start | bytes 2097152 | tf_op jit(solution)/shard_map/all_to_all | solution.py:38
  67.2 211.4 %all-reduce.3.cloned.1.call-start = ((), (), s32[]{:S(2)}) async-start(), calls=%async_computation.2 | async-start | bytes 4194304 | tf_op jit(solution)/shard_map/psum | solution.py:57
  95.4 1.3 copy-start.3
  96.9 10.4 %collective-permute-start = (bf16[2,64,1,512]{3,1,2,0:T(8,128)(2,1)S(1)}, bf16[2,64,1,512]{3,1,2,0:T(8,128)(2,1)S(1)}, u32[]{:S(2)}, u32[]{:S(2)}) collective-permute-start(bf16[2,64,1,512]{3,1,2,0:T(8,128)(2,1)S(1)} %copy.119), channel_id=1, source_target_pairs={{32,0},{64,32},{96,64},{128,96},{160,128},{192,160},{224,192},{256... | collective-permute-start | bytes 393224 | tf_op jit(solution)/shard_map/ppermute | solution.py:14
  100.4 3.2 copy-start.4
  106.9 1.9 copy-start.7
  107.3 3.0 copy-start.9
  108.8 1.5 copy-start.11
  108.8 1.5 copy-start.13
  113.8 0.7 copy-start.15
  278.6 3.1 copy-start.1
  283.6 1.3 copy-start.5
  558.0 1.3 copy-start.2
  726.9 4.9 copy-start.8
  726.9 4.9 copy-start.10
  726.9 4.9 copy-start.12
  726.9 4.9 copy-start.14
  731.8 1.6 copy-start.6
Sparse Core Ops, SparseCore 0:
  113.9 164.6 all-reduce.2
where the time goes:
time: 742 us
  other arithmetic  434 us (58%)
  waiting for transfers between devices  212 us (29%)
  local copies, waits for them, and re-layouts  44.3 us (6%)
  starting transfers between devices  20.5 us (3%)
  matrix products  15.5 us (2%)
  between operations  14.5 us (2%)
    another operation x10, other arithmetic, shards(): lower = jnp.linalg.cholesky(covariance)  268 us
    psum x1, waiting for transfers between devices, shards(): covariance = lax.psum(local, 'rng')  164 us
    another operation x5, other arithmetic, shards(): lax.linalg.triangular_solve(lower, first, left_side=True, lower=True, tra...  162 us
    all_to_all x1, waiting for transfers between devices, shards(): lax.all_to_all(spectra(pulse_block, table), 'dop', split_axis=2, concat_a...  24.2 us
    all_to_all x1, waiting for transfers between devices, shards(): lax.all_to_all(cube, 'dop', split_axis=3, concat_axis=2, tiled=True)  24 us
    unnamed x45, local copies, waits for them, and re-layouts  19.4 us
  transfers between devices with their start and end apart: 4, of which 3 were waited for; matrix products, arithmetic and copies ran while one was open for 1% of the time, Pallas kernels for 0%

commit v1 on v0

--- a/solution.py
+++ b/solution.py
@@ -54,7 +54,11 @@
     top = jnp.concatenate([real_part, -cross], axis=2)
     bottom = jnp.concatenate([cross, real_part], axis=2)
     local = jnp.concatenate([top, bottom], axis=1) + prior_gram
-    covariance = lax.psum(local, "rng")
+    covariance = local
+    for hop in (1, 2, 4, 8, 16):
+        covariance = covariance + lax.ppermute(
+            covariance, "rng", [(dev, dev ^ hop) for dev in range(32)]
+        )
     lower = jnp.linalg.cholesky(covariance)
     first = lax.linalg.triangular_solve(lower, steering[:, :, None], left_side=True, lower=True)
     second = lax.linalg.triangular_solve(lower, first, left_side=True, lower=True, transpose_a=True)

time: 742 us -> 907 us (1.22)
  the two profiles are of different devices: /device:TPU:64 before, /device:TPU:56 now
where the time goes in v1:
time: 907 us; the launch traced here: 906 us
  other arithmetic  438 us (48%)
  waiting for transfers between devices  374 us (41%)
  local copies, waits for them, and re-layouts  42.4 us (5%)
  starting transfers between devices  36.5 us (4%)
  matrix products  14.2 us (2%)
    ppermute x5, waiting for transfers between devices, shards(): lax.ppermute(covariance, 'rng', [(dev, dev ^ hop) for dev in range(32)])  322 us
    another operation x10, other arithmetic, shards(): lower = jnp.linalg.cholesky(covariance)  268 us
    another operation x5, other arithmetic, shards(): lax.linalg.triangular_solve(lower, first, left_side=True, lower=True, tra...  161 us
    all_to_all x1, waiting for transfers between devices, shards(): lax.all_to_all(spectra(pulse_block, table), 'dop', split_axis=2, concat_a...  26.3 us
    all_to_all x1, waiting for transfers between devices, shards(): lax.all_to_all(cube, 'dop', split_axis=3, concat_axis=2, tiled=True)  25.9 us
    ppermute x5, starting transfers between devices, shards(): lax.ppermute(covariance, 'rng', [(dev, dev ^ hop) for dev in range(32)])  20.4 us
    unnamed x47, local copies, waits for them, and re-layouts  18.8 us
  transfers between devices with their start and end apart: 8, of which 7 were waited for; matrix products, arithmetic and copies ran while one was open for 1% of the time, Pallas kernels for 0%

profile of v1, /device:TPU:56, one launch (start us, length us, event | category | flops | bytes accessed | tf_op | source)
XLA Modules:
  0.0 906.2 jit_solution(13544701861242480445)
XLA Ops:
  0.6 4.0 copy.72
  6.9 10.4 %all-to-all-start = ((bf16[16,2,16384]{2,1,0:T(2,128)(2,1)}), bf16[16,2,16384]{2,1,0:T(2,128)(2,1)S(1)}, u32[]{:S(2)}, u32[]{:S(2)}) async-start(bf16[16,2,16384]{2,1,0:T(2,128)(2,1)} %reshape.203), calls=%async_computation | async-start | bytes 2097152 | tf_op jit(solution)/shard_map/all_to_all | solution.py:37
  17.9 25.9 %all-to-all-done = bf16[16,2,16384]{2,1,0:T(2,128)(2,1)S(1)} async-done(((bf16[16,2,16384]{2,1,0:T(2,128)(2,1)}), bf16[16,2,16384]{2,1,0:T(2,128)(2,1)S(1)}, u32[]{:S(2)}, u32[]{:S(2)}) %all-to-all-start) | async-done | bytes 1048608 | tf_op jit(solution)/shard_map/all_to_all | solution.py:37
  50.9 3.0 copy.76
  56.2 4.9 all-to-all-start.1
  61.3 26.3 %all-to-all-done.1 = bf16[16,2,16384]{2,1,0:T(2,128)(2,1)S(1)} async-done(((bf16[16,2,16384]{2,1,0:T(2,128)(2,1)}), bf16[16,2,16384]{2,1,0:T(2,128)(2,1)S(1)}, u32[]{:S(2)}, u32[]{:S(2)}) %all-to-all-start.1) | async-done | bytes 1048608 | tf_op jit(solution)/shard_map/all_to_all | solution.py:38
  93.4 3.2 fusion.42
  105.5 3.2 collective-permute-start.1
  108.8 46.9 %collective-permute-done.1 = f32[8,256,256]{1,2,0:T(8,128)S(1)} collective-permute-done((f32[8,256,256]{1,2,0:T(8,128)S(1)}, f32[8,256,256]{1,2,0:T(8,128)S(1)}, u32[]{:S(2)}, u32[]{:S(2)}) %collective-permute-start.1) | collective-permute-done | bytes 2097184 | tf_op jit(solution)/shard_map/ppermute | solution.py:59
  156.0 4.0 collective-permute-start.2
  160.0 91.3 %collective-permute-done.2 = f32[8,256,256]{1,2,0:T(8,128)S(1)} collective-permute-done((f32[8,256,256]{1,2,0:T(8,128)S(1)}, f32[8,256,256]{1,2,0:T(8,128)S(1)}, u32[]{:S(2)}, u32[]{:S(2)}) %collective-permute-start.2) | collective-permute-done | bytes 2097184 | tf_op jit(solution)/shard_map/ppermute | solution.py:59
  251.7 4.6 collective-permute-start.3
  256.3 92.9 %collective-permute-done.3 = f32[8,256,256]{1,2,0:T(8,128)S(1)} collective-permute-done((f32[8,256,256]{1,2,0:T(8,128)S(1)}, f32[8,256,256]{1,2,0:T(8,128)S(1)}, u32[]{:S(2)}, u32[]{:S(2)}) %collective-permute-start.3) | collective-permute-done | bytes 2097184 | tf_op jit(solution)/shard_map/ppermute | solution.py:59
  349.5 3.4 collective-permute-start.4
  352.9 46.0 %collective-permute-done.4 = f32[8,256,256]{1,2,0:T(8,128)S(1)} collective-permute-done((f32[8,256,256]{1,2,0:T(8,128)S(1)}, f32[8,256,256]{1,2,0:T(8,128)S(1)}, u32[]{:S(2)}, u32[]{:S(2)}) %collective-permute-start.4) | collective-permute-done | bytes 2097184 | tf_op jit(solution)/shard_map/ppermute | solution.py:59
  399.2 5.1 collective-permute-start.5
  404.5 44.8 %collective-permute-done.5 = f32[8,256,256]{1,2,0:T(8,128)} collective-permute-done((f32[8,256,256]{1,2,0:T(8,128)S(1)}, f32[8,256,256]{1,2,0:T(8,128)}, u32[]{:S(2)}, u32[]{:S(2)}) %collective-permute-start.5) | collective-permute-done | bytes 2097184 | tf_op jit(solution)/shard_map/ppermute | solution.py:59
  457.0 93.8 %custom-call.18 = f32[8,128,128]{2,1,0:T(8,128)S(1)} custom-call(f32[8,128,128]{2,1,0:T(8,128)S(1)} %cholesky.122), custom_call_target="Cholesky" | custom-call | tf_op jit(solution)/shard_map/jit(cholesky)/cholesky | solution.py:62
  551.0 79.2 %custom-call.19 = f32[8,1,128,128]{2,3,1,0:T(8,128)} custom-call(f32[8,1,128,128]{3,2,1,0:T(8,128)S(1)} %select_bitcast_fusion), custom_call_target="InvertDiagBlocksLowerTriangular" | custom-call | tf_op jit(solution)/shard_map/jit(cholesky)/cholesky | solution.py:62
  632.1 3.1 slice_subtract_fusion
  635.1 94.6 %custom-call.20 = f32[8,128,128]{2,1,0:T(8,128)S(1)} custom-call(f32[8,128,128]{2,1,0:T(8,128)} %slice_subtract_fusion), custom_call_target="Cholesky" | custom-call | tf_op jit(solution)/shard_map/jit(cholesky)/cholesky | solution.py:62
  731.1 3.4 broadcast_select_fusion
  734.6 5.8 while.1
  740.4 158.0 %custom-call.21 = f32[8,2,128,128]{2,3,1,0:T(8,128)S(1)} custom-call(f32[8,2,128,128]{3,2,1,0:T(8,128)} %bitcast.155), custom_call_target="InvertDiagBlocksLowerTriangular" | custom-call | tf_op jit(solution)/shard_map/triangular_solve | solution.py:64
  (113 shorter events, 52.6 us)
Async XLA Ops:
  0.6 102.9 %copy-start = (f32[8,8,256]{2,1,0:T(8,128)S(1)}, f32[8,8,256]{2,1,0:T(8,128)}, u32[]{:S(2)}) copy-start(f32[8,8,256]{2,1,0:T(8,128)} %param.8) | copy-start | bytes 196612
  6.9 36.9 %all-to-all-start = ((bf16[16,2,16384]{2,1,0:T(2,128)(2,1)}), bf16[16,2,16384]{2,1,0:T(2,128)(2,1)S(1)}, u32[]{:S(2)}, u32[]{:S(2)}) async-start(bf16[16,2,16384]{2,1,0:T(2,128)(2,1)} %reshape.203), calls=%async_computation | async-start | bytes 2097152 | tf_op jit(solution)/shard_map/all_to_all | solution.py:37
  53.9 7.2 copy-start.17
  53.9 7.2 copy-start.18
  56.2 31.4 %all-to-all-start.1 = ((bf16[16,2,16384]{2,1,0:T(2,128)(2,1)}), bf16[16,2,16384]{2,1,0:T(2,128)(2,1)S(1)}, u32[]{:S(2)}, u32[]{:S(2)}) async-start(bf16[16,2,16384]{2,1,0:T(2,128)(2,1)} %reshape.205), calls=%async_computation.1 | async-start | bytes 2097152 | tf_op jit(solution)/shard_map/all_to_all | solution.py:38
  92.7 7.7 collective-permute-start
  93.4 3.2 copy-start.5
  99.9 1.9 copy-start.8
  100.4 3.0 copy-start.10
  101.8 1.5 copy-start.12
  101.8 1.5 copy-start.14
  105.5 50.2 %collective-permute-start.1 = (f32[8,256,256]{1,2,0:T(8,128)S(1)}, f32[8,256,256]{1,2,0:T(8,128)S(1)}, u32[]{:S(2)}, u32[]{:S(2)}) collective-permute-start(f32[8,256,256]{1,2,0:T(8,128)S(1)} %maximum_add_fusion), channel_id=1, source_target_pairs={{0,1},{1,0},{2,3},{3,2},{4,5},{5,4},{6,7},{7,6},{8,9},{9,8},{10,11... | collective-permute-start | bytes 6291464 | tf_op jit(solution)/shard_map/ppermute | solution.py:59
  156.0 95.4 %collective-permute-start.2 = (f32[8,256,256]{1,2,0:T(8,128)S(1)}, f32[8,256,256]{1,2,0:T(8,128)S(1)}, u32[]{:S(2)}, u32[]{:S(2)}) collective-permute-start(f32[8,256,256]{1,2,0:T(8,128)S(1)} %add.78), channel_id=1, source_target_pairs={{0,2},{1,3},{2,0},{3,1},{4,6},{5,7},{6,4},{7,5},{8,10},{9,11},{10,... | collective-permute-start | bytes 6291464 | tf_op jit(solution)/shard_map/ppermute | solution.py:59
  251.7 97.5 %collective-permute-start.3 = (f32[8,256,256]{1,2,0:T(8,128)S(1)}, f32[8,256,256]{1,2,0:T(8,128)S(1)}, u32[]{:S(2)}, u32[]{:S(2)}) collective-permute-start(f32[8,256,256]{1,2,0:T(8,128)S(1)} %add.79), channel_id=1, source_target_pairs={{0,4},{1,5},{2,6},{3,7},{4,0},{5,1},{6,2},{7,3},{8,12},{9,13},{10,... | collective-permute-start | bytes 6291464 | tf_op jit(solution)/shard_map/ppermute | solution.py:59
  349.5 54.9 %copy-start.16 = (f32[8,256]{1,0:T(8,128)S(1)}, f32[8,256]{1,0:T(8,128)}, u32[]{:S(2)}) copy-start(f32[8,256]{1,0:T(8,128)} %param.9) | copy-start | bytes 24580
  349.5 49.4 %collective-permute-start.4 = (f32[8,256,256]{1,2,0:T(8,128)S(1)}, f32[8,256,256]{1,2,0:T(8,128)S(1)}, u32[]{:S(2)}, u32[]{:S(2)}) collective-permute-start(f32[8,256,256]{1,2,0:T(8,128)S(1)} %add.80), channel_id=1, source_target_pairs={{0,8},{1,9},{2,10},{3,11},{4,12},{5,13},{6,14},{7,15},{8,0},{9,1},... | collective-permute-start | bytes 6291464 | tf_op jit(solution)/shard_map/ppermute | solution.py:59
  399.2 5.3 copy-start.2
  399.2 50.1 %collective-permute-start.5 = (f32[8,256,256]{1,2,0:T(8,128)S(1)}, f32[8,256,256]{1,2,0:T(8,128)}, u32[]{:S(2)}, u32[]{:S(2)}) collective-permute-start(f32[8,256,256]{1,2,0:T(8,128)S(1)} %add.81), channel_id=1, source_target_pairs={{0,16},{1,17},{2,18},{3,19},{4,20},{5,21},{6,22},{7,23},{8,24},{9,... | collective-permute-start | bytes 6291464 | tf_op jit(solution)/shard_map/ppermute | solution.py:59
  898.4 4.9 copy-start.9
  898.4 4.9 copy-start.11
  898.4 4.9 copy-start.13
  898.4 4.9 copy-start.15
  903.3 1.6 copy-start.7
  903.3 2.9 copy-start.1
  (3 other events, 4.0 us)
